TPU v7x, 32 devices: a whole 2x2x4 slice. The times are simulated.
32 devices in a mesh: dp: 16 (over z, y, core), ctx: 2 (over x).
Axes of the slice: x: 2, y: 2, z: 4, core: 2. Of those that a mesh axis runs over, the one named last changes fastest.
Arguments:
- conv_input: bfloat16 [16, 256, 4096], P('dp', 'ctx'), may hold values from -6 to 6
- gate_value: bfloat16 [16, 256, 4096], P('dp', 'ctx'), may hold values from -6 to 6
- out_grad: bfloat16 [16, 256, 4096], P('dp', 'ctx'), may hold values from -6 to 6
- filter_taps: bfloat16 [128, 4096], P('dp'), may hold values from -0.5 to 0.5
Outputs:
- input_grad: bfloat16 [16, 256, 4096], P('dp', 'ctx')
- filter_grad: float32 [128, 4096], P('dp')
All inputs are finite; a program needn't handle non-finite values.
Results may differ from a plain program's by a relative error of at most 0.0051.
Values may be sent and summed in bfloat16 or wider, within the bound.
A program may use at most 64 MiB of HBM per device.

v0:
```python
import math
import jax
import jax.numpy as jnp
from jax import lax
from jax.sharding import PartitionSpec as P

TAPS = 128


def from_behind(block, axis, distance):
    devices = range(lax.axis_size(axis))
    route = [(i - distance, i) for i in devices if i - distance in devices]
    return lax.ppermute(block, axis, route)


def correlate(signal, kernel):
    return lax.conv_general_dilated(
        signal[None],
        kernel[:, None, :],
        (1,),
        "VALID",
        dimension_numbers=("NWC", "WIO", "NWC"),
        feature_group_count=signal.shape[1],
        preferred_element_type=jnp.float32,
    )[0]


def shards(conv_input, gate_value, out_grad, filter_taps):
    inputs = conv_input[0]
    rows = inputs.shape[0]
    mixed = (out_grad[0].astype(jnp.float32) * gate_value[0].astype(jnp.float32)).astype(
        jnp.bfloat16
    )
    rim_rows = from_behind(mixed[: TAPS - 1], "ctx", -1)
    grad_ext = jnp.concatenate([mixed, rim_rows], 0)
    partial_grad = correlate(grad_ext, inputs)
    full_taps = lax.all_gather(filter_taps, "dp", axis=0, tiled=True)
    back_sum = correlate(grad_ext, full_taps)
    summed = lax.psum(partial_grad, "ctx")
    shard_grad = lax.psum_scatter(summed, "dp", scatter_dimension=0, tiled=True)
    tokens_all = rows * lax.axis_size("ctx") * lax.axis_size("dp")
    scale_factor = 1.0 / math.sqrt(tokens_all)
    return (back_sum.astype(jnp.bfloat16)[None], shard_grad * scale_factor)


def solution(mesh):
    in_specs = (P("dp", "ctx", None), P("dp", "ctx", None), P("dp", "ctx", None), P("dp", None))
    out_specs = (P("dp", "ctx", None), P("dp", None))
    return jax.shard_map(shards, mesh=mesh, in_specs=in_specs, out_specs=out_specs, check_vma=False)
```

profile of v0, /device:TPU:0, one launch (start us, length us, event | category | flops | bytes accessed | tf_op | source)
XLA Modules:
  0.0 211.5 jit_solution(7849527368872966788)
XLA Ops:
  7.2 0.0 copy-start
  7.2 0.0 reduce-scatter.2.cloned.1.call-start
  7.2 1.9 multiply_convert_fusion
  9.2 0.1 slice_bitcast_fusion
  9.2 1.3 collective-permute-start
  10.5 26.2 %collective-permute-done = bf16[127,4096]{1,0:T(8,128)(2,1)S(1)} collective-permute-done((bf16[127,4096]{1,0:T(8,128)(2,1)S(1)}, bf16[127,4096]{1,0:T(8,128)(2,1)S(1)}, u32[]{:S(2)}, u32[]{:S(2)}) %collective-permute-start) | collective-permute-done | bytes 1040416 | tf_op jit(solution)/shard_map/ppermute | solution.py:13
  36.7 0.2 maximum_bitcast_fusion
  36.9 0.0 copy-done
  36.9 30.1 %fusion = f32[1,128,4096]{2,0,1:T(1,128)S(1)} fusion(bf16[1,255,4096]{2,1,0:T(8,128)(2,1)S(1)} %maximum_bitcast_fusion, bf16[128,1,4096]{2,0,1:T(8,128)(2,1)S(1)} %bitcast.10), kind=kOutput, calls=%fused_computation.1 | convolution fusion | flops 134217728 | bytes 5234688 | tf_op jit(solution)/shard_map/conv_general_dilated | solution.py:17
  67.0 3.0 %copy.23 = f32[1,128,4096]{2,1,0:T(8,128)} copy(f32[1,128,4096]{2,0,1:T(1,128)S(1)} %fusion) | data formatting | bytes 4194304
  70.0 0.0 reduce-scatter.2.cloned.1.call-update
  70.0 0.0 all-gather.2.cloned.1.call-start
  70.1 0.7 all-gather.2.cloned.1.call-update
  70.8 0.0 all-reduce.2.cloned.1.call-start
  70.8 62.3 %reduce-scatter.2.cloned.1.call-done = f32[8,4096]{1,0:T(8,128)} async-done(((f32[128,4096]{1,0:T(8,128)}), f32[8,4096]{1,0:T(8,128)}) %reduce-scatter.2.cloned.1.call-update) | async-done | bytes 131088 | tf_op jit(solution)/shard_map/reduce_scatter | solution.py:40
  133.1 0.0 all-reduce.2.cloned.1.call-update
  133.2 39.0 %all-gather.2.cloned.1.call-done = bf16[128,4096]{1,0:T(8,128)(2,1)} async-done(((bf16[8,4096]{1,0:T(8,128)(2,1)}), bf16[128,4096]{1,0:T(8,128)(2,1)}) %all-gather.2.cloned.1.call-update) | async-done | bytes 1048592 | tf_op jit(solution)/shard_map/all_gather | solution.py:37
  172.2 29.1 %convolution_convert_fusion = bf16[1,128,4096]{2,0,1:T(2,128)(2,1)S(1)} fusion(bf16[1,255,4096]{2,1,0:T(8,128)(2,1)S(1)} %maximum_bitcast_fusion, bf16[128,1,4096]{2,0,1:T(8,128)(2,1)} %bitcast.13), kind=kOutput, calls=%fused_computation | convolution fusion | flops 134742016 | bytes 4186112 | tf_op jit(solution)/shard_map/conv_general_dilated | solution.py:17
  201.3 2.1 copy.12
  203.4 0.0 all-reduce.2.cloned.1.call-done
  203.4 1.6 broadcast_multiply_fusion
Async XLA Ops:
  7.2 29.8 %copy-start = (bf16[1,128,4096]{2,1,0:T(8,128)(2,1)S(1)}, bf16[1,128,4096]{2,1,0:T(8,128)(2,1)}, u32[]{:S(2)}) copy-start(bf16[1,128,4096]{2,1,0:T(8,128)(2,1)} %param.4) | copy-start | bytes 3145732
  7.2 126.0 %reduce-scatter.2.cloned.1.call-start = ((), (), s32[]{:S(2)}) async-start(), calls=%async_computation.2 | async-start | bytes 2228224 | tf_op jit(solution)/shard_map/reduce_scatter | solution.py:40
  9.2 27.5 %collective-permute-start = (bf16[127,4096]{1,0:T(8,128)(2,1)S(1)}, bf16[127,4096]{1,0:T(8,128)(2,1)S(1)}, u32[]{:S(2)}, u32[]{:S(2)}) collective-permute-start(bf16[127,4096]{1,0:T(8,128)(2,1)S(1)} %slice_bitcast_fusion), channel_id=1, source_target_pairs={{1,0},{3,2},{5,4},{7,6},{9,8},{11,10},{13,12},{15,14},{17,16},{19,... | collective-permute-start | bytes 3121160 | tf_op jit(solution)/shard_map/ppermute | solution.py:13
  70.0 102.1 %all-gather.2.cloned.1.call-start = ((), (), s32[]{:S(2)}) async-start(), calls=%async_computation.1 | async-start | bytes 1114112 | tf_op jit(solution)/shard_map/all_gather | solution.py:37
  70.8 132.6 %all-reduce.2.cloned.1.call-start = ((), (), s32[]{:S(2)}) async-start(), calls=%async_computation.3 | async-start | bytes 262144 | tf_op jit(solution)/shard_map/psum | solution.py:39
Sparse Core Ops, SparseCore 0:
  70.2 62.9 reduce-scatter.1
  135.3 36.8 all-gather.1
  174.4 20.4 all-reduce.1
where the time goes:
time: 212 us; the launch traced here: 211 us
  waiting for transfers between devices  128 us (60%)
  matrix products  59.2 us (28%)
  between operations  13.8 us (7%)
  local copies, waits for them, and re-layouts  5.18 us (2%)
  other arithmetic  3.71 us (2%)
    reduce_scatter x1, waiting for transfers between devices, shards(): shard_grad = lax.psum_scatter(summed, 'dp', scatter_dimension=0, tiled=True)  62.3 us
    conv_general_dilated x2, matrix products, correlate(): lax.conv_general_dilated(signal[None], kernel[:, None, :], (1,), 'VALID',...  59.2 us
    all_gather x1, waiting for transfers between devices, shards(): full_taps = lax.all_gather(filter_taps, 'dp', axis=0, tiled=True)  39 us
    ppermute x1, waiting for transfers between devices, from_behind(): return lax.ppermute(block, axis, route)  26.2 us
    unnamed x4, local copies, waits for them, and re-layouts  5.1 us
  transfers between devices with their start and end apart: 4, of which 3 were waited for; matrix products, arithmetic and copies ran while one was open for 15% of the time, Pallas kernels for 0%

commit v1 on v0

--- a/solution.py
+++ b/solution.py
@@ -1,3 +1,4 @@
+import functools
 import math
 import jax
 import jax.numpy as jnp
@@ -5,6 +6,20 @@
 from jax.sharding import PartitionSpec as P
 
 TAPS = 128
+
+
+def _lift_stops_all(xx, on_dim):
+    size_here = lax.axis_size("dp")
+    pile = tuple(((idx, (idx + 1) % size_here) for idx in range(size_here)))
+    heard = [None] * size_here
+    heard[size_here - 1] = xx
+    for k0 in range(size_here - 2, -1, -1):
+        heard[k0] = lax.ppermute(heard[k0 + 1], perm=pile, axis_name="dp")
+    response = jnp.concatenate(heard, on_dim)
+    return jnp.roll(response, (lax.axis_index("dp") + 1) * xx.shape[on_dim], axis=on_dim)
+
+
+expand_waves = functools.partial(_lift_stops_all, on_dim=0)
 
 
 def from_behind(block, axis, distance):
@@ -34,7 +49,7 @@
     rim_rows = from_behind(mixed[: TAPS - 1], "ctx", -1)
     grad_ext = jnp.concatenate([mixed, rim_rows], 0)
     partial_grad = correlate(grad_ext, inputs)
-    full_taps = lax.all_gather(filter_taps, "dp", axis=0, tiled=True)
+    full_taps = expand_waves(filter_taps)
     back_sum = correlate(grad_ext, full_taps)
     summed = lax.psum(partial_grad, "ctx")
     shard_grad = lax.psum_scatter(summed, "dp", scatter_dimension=0, tiled=True)

time: 212 us -> 259 us (1.22)
  waiting for transfers between devices: 128 us -> 156 us
  local copies, waits for them, and re-layouts: 5.18 us -> 21.5 us
    ppermute x0 -> x15, waiting for transfers between devices: none -> 93.6 us  [_lift_stops_all(): heard[k0] = lax.ppermute(heard[k0 + 1], perm=pile, axis_name='dp')]
    all_gather x1 -> x0, waiting for transfers between devices: 39 us -> none  [shards(): full_taps = lax.all_gather(filter_taps, 'dp', axis=0, tiled=True)]
    ppermute x1, waiting for transfers between devices: 26.2 us -> 4.95 us  [from_behind(): return lax.ppermute(block, axis, route)]
    unnamed x4 -> x75, local copies, waits for them, and re-layouts: 5.1 us -> 18.5 us
    reduce_scatter x1, waiting for transfers between devices: 62.3 us -> 57.4 us  [shards(): shard_grad = lax.psum_scatter(summed, 'dp', scatter_dimension=0, tiled=True)]
  transfers between devices with their start and end apart: 4 -> 18, of which waited for: 3 -> 17; matrix products, arithmetic and copies ran while one was open for 15% -> 19% of each run, Pallas kernels for 0% -> 0%
where the time goes in v1:
time: 259 us; the launch traced here: 258 us
  waiting for transfers between devices  156 us (60%)
  matrix products  59.2 us (23%)
  local copies, waits for them, and re-layouts  21.5 us (8%)
  between operations  14.5 us (6%)
  other arithmetic  4.76 us (2%)
    ppermute x15, waiting for transfers between devices, _lift_stops_all(): heard[k0] = lax.ppermute(heard[k0 + 1], perm=pile, axis_name='dp')  93.6 us
    conv_general_dilated x2, matrix products, correlate(): lax.conv_general_dilated(signal[None], kernel[:, None, :], (1,), 'VALID',...  59.2 us
    reduce_scatter x1, waiting for transfers between devices, shards(): shard_grad = lax.psum_scatter(summed, 'dp', scatter_dimension=0, tiled=True)  57.4 us
    unnamed x75, local copies, waits for them, and re-layouts  18.5 us
  transfers between devices with their start and end apart: 18, of which 17 were waited for; matrix products, arithmetic and copies ran while one was open for 19% of the time, Pallas kernels for 0%

profile of v1, /device:TPU:0, one launch (start us, length us, event | category | flops | bytes accessed | tf_op | source)
XLA Modules:
  0.0 258.0 jit_solution(8226032722990518492)
XLA Ops:
  7.8 7.1 %collective-permute-done.1 = bf16[8,4096]{1,0:T(8,128)(2,1)S(1)} collective-permute-done((bf16[8,4096]{1,0:T(8,128)(2,1)}, bf16[8,4096]{1,0:T(8,128)(2,1)S(1)}, u32[]{:S(2)}, u32[]{:S(2)}) %collective-permute-start.1) | collective-permute-done | bytes 65568 | tf_op jit(solution)/shard_map/ppermute | solution.py:17
  14.9 6.4 %collective-permute-done.2 = bf16[8,4096]{1,0:T(8,128)(2,1)S(1)} collective-permute-done((bf16[8,4096]{1,0:T(8,128)(2,1)S(1)}, bf16[8,4096]{1,0:T(8,128)(2,1)S(1)}, u32[]{:S(2)}, u32[]{:S(2)}) %collective-permute-start.2) | collective-permute-done | bytes 65568 | tf_op jit(solution)/shard_map/ppermute | solution.py:17
  21.3 6.4 %collective-permute-done.3 = bf16[8,4096]{1,0:T(8,128)(2,1)S(1)} collective-permute-done((bf16[8,4096]{1,0:T(8,128)(2,1)S(1)}, bf16[8,4096]{1,0:T(8,128)(2,1)S(1)}, u32[]{:S(2)}, u32[]{:S(2)}) %collective-permute-start.3) | collective-permute-done | bytes 65568 | tf_op jit(solution)/shard_map/ppermute | solution.py:17
  27.7 6.4 %collective-permute-done.4 = bf16[8,4096]{1,0:T(8,128)(2,1)S(1)} collective-permute-done((bf16[8,4096]{1,0:T(8,128)(2,1)S(1)}, bf16[8,4096]{1,0:T(8,128)(2,1)S(1)}, u32[]{:S(2)}, u32[]{:S(2)}) %collective-permute-start.4) | collective-permute-done | bytes 65568 | tf_op jit(solution)/shard_map/ppermute | solution.py:17
  34.1 6.4 %collective-permute-done.5 = bf16[8,4096]{1,0:T(8,128)(2,1)S(1)} collective-permute-done((bf16[8,4096]{1,0:T(8,128)(2,1)S(1)}, bf16[8,4096]{1,0:T(8,128)(2,1)S(1)}, u32[]{:S(2)}, u32[]{:S(2)}) %collective-permute-start.5) | collective-permute-done | bytes 65568 | tf_op jit(solution)/shard_map/ppermute | solution.py:17
  40.5 6.4 %collective-permute-done.6 = bf16[8,4096]{1,0:T(8,128)(2,1)S(1)} collective-permute-done((bf16[8,4096]{1,0:T(8,128)(2,1)S(1)}, bf16[8,4096]{1,0:T(8,128)(2,1)S(1)}, u32[]{:S(2)}, u32[]{:S(2)}) %collective-permute-start.6) | collective-permute-done | bytes 65568 | tf_op jit(solution)/shard_map/ppermute | solution.py:17
  46.9 6.4 %collective-permute-done.7 = bf16[8,4096]{1,0:T(8,128)(2,1)S(1)} collective-permute-done((bf16[8,4096]{1,0:T(8,128)(2,1)S(1)}, bf16[8,4096]{1,0:T(8,128)(2,1)S(1)}, u32[]{:S(2)}, u32[]{:S(2)}) %collective-permute-start.7) | collective-permute-done | bytes 65568 | tf_op jit(solution)/shard_map/ppermute | solution.py:17
  53.3 6.4 %collective-permute-done.8 = bf16[8,4096]{1,0:T(8,128)(2,1)S(1)} collective-permute-done((bf16[8,4096]{1,0:T(8,128)(2,1)S(1)}, bf16[8,4096]{1,0:T(8,128)(2,1)S(1)}, u32[]{:S(2)}, u32[]{:S(2)}) %collective-permute-start.8) | collective-permute-done | bytes 65568 | tf_op jit(solution)/shard_map/ppermute | solution.py:17
  59.6 6.4 %collective-permute-done.9 = bf16[8,4096]{1,0:T(8,128)(2,1)S(1)} collective-permute-done((bf16[8,4096]{1,0:T(8,128)(2,1)S(1)}, bf16[8,4096]{1,0:T(8,128)(2,1)S(1)}, u32[]{:S(2)}, u32[]{:S(2)}) %collective-permute-start.9) | collective-permute-done | bytes 65568 | tf_op jit(solution)/shard_map/ppermute | solution.py:17
  66.0 6.4 %collective-permute-done.10 = bf16[8,4096]{1,0:T(8,128)(2,1)S(1)} collective-permute-done((bf16[8,4096]{1,0:T(8,128)(2,1)S(1)}, bf16[8,4096]{1,0:T(8,128)(2,1)S(1)}, u32[]{:S(2)}, u32[]{:S(2)}) %collective-permute-start.10) | collective-permute-done | bytes 65568 | tf_op jit(solution)/shard_map/ppermute | solution.py:17
  72.4 6.4 %collective-permute-done.11 = bf16[8,4096]{1,0:T(8,128)(2,1)S(1)} collective-permute-done((bf16[8,4096]{1,0:T(8,128)(2,1)S(1)}, bf16[8,4096]{1,0:T(8,128)(2,1)S(1)}, u32[]{:S(2)}, u32[]{:S(2)}) %collective-permute-start.11) | collective-permute-done | bytes 65568 | tf_op jit(solution)/shard_map/ppermute | solution.py:17
  78.8 6.4 %collective-permute-done.12 = bf16[8,4096]{1,0:T(8,128)(2,1)S(1)} collective-permute-done((bf16[8,4096]{1,0:T(8,128)(2,1)S(1)}, bf16[8,4096]{1,0:T(8,128)(2,1)S(1)}, u32[]{:S(2)}, u32[]{:S(2)}) %collective-permute-start.12) | collective-permute-done | bytes 65568 | tf_op jit(solution)/shard_map/ppermute | solution.py:17
  85.2 6.4 %collective-permute-done.13 = bf16[8,4096]{1,0:T(8,128)(2,1)S(1)} collective-permute-done((bf16[8,4096]{1,0:T(8,128)(2,1)S(1)}, bf16[8,4096]{1,0:T(8,128)(2,1)S(1)}, u32[]{:S(2)}, u32[]{:S(2)}) %collective-permute-start.13) | collective-permute-done | bytes 65568 | tf_op jit(solution)/shard_map/ppermute | solution.py:17
  91.7 1.8 multiply_convert_fusion
  93.5 4.7 %collective-permute-done.14 = bf16[8,4096]{1,0:T(8,128)(2,1)} collective-permute-done((bf16[8,4096]{1,0:T(8,128)(2,1)S(1)}, bf16[8,4096]{1,0:T(8,128)(2,1)}, u32[]{:S(2)}, u32[]{:S(2)}) %collective-permute-start.14) | collective-permute-done | bytes 65568 | tf_op jit(solution)/shard_map/ppermute | solution.py:17
  98.3 1.3 collective-permute-start
  99.7 5.2 %collective-permute-done.15 = bf16[8,4096]{1,0:T(8,128)(2,1)} collective-permute-done((bf16[8,4096]{1,0:T(8,128)(2,1)}, bf16[8,4096]{1,0:T(8,128)(2,1)}, u32[]{:S(2)}, u32[]{:S(2)}) %collective-permute-start.15) | collective-permute-done | bytes 65568 | tf_op jit(solution)/shard_map/ppermute | solution.py:17
  104.9 0.8 constant_dynamic-update-slice_fusion.31
  107.4 0.8 constant_dynamic-update-slice_fusion.28
  109.1 0.8 constant_dynamic-update-slice_fusion.26
  110.8 0.8 constant_dynamic-update-slice_fusion.24
  112.5 0.8 constant_dynamic-update-slice_fusion.22
  113.4 0.8 constant_dynamic-update-slice_fusion.15
  115.3 5.0 %collective-permute-done = bf16[127,4096]{1,0:T(8,128)(2,1)} collective-permute-done((bf16[127,4096]{1,0:T(8,128)(2,1)S(1)}, bf16[127,4096]{1,0:T(8,128)(2,1)}, u32[]{:S(2)}, u32[]{:S(2)}) %collective-permute-start) | collective-permute-done | bytes 1040416 | tf_op jit(solution)/shard_map/ppermute | solution.py:28
  120.3 1.4 maximum_bitcast_fusion
  121.7 30.1 %fusion = f32[1,128,4096]{2,0,1:T(1,128)S(1)} fusion(bf16[1,255,4096]{2,1,0:T(8,128)(2,1)S(1)} %maximum_bitcast_fusion, bf16[128,1,4096]{2,0,1:T(8,128)(2,1)S(1)} %bitcast.11), kind=kOutput, calls=%fused_computation.1 | convolution fusion | flops 134217728 | bytes 5234688 | tf_op jit(solution)/shard_map/conv_general_dilated | solution.py:32
  151.8 3.0 %copy.23 = f32[1,128,4096]{2,1,0:T(8,128)} copy(f32[1,128,4096]{2,0,1:T(1,128)S(1)} %fusion) | data formatting | bytes 4194304
  158.6 2.3 dynamic-slice_bitcast_fusion
  160.9 57.4 %reduce-scatter.2.cloned.1.call-done = f32[8,4096]{1,0:T(8,128)} async-done(((f32[128,4096]{1,0:T(8,128)}), f32[8,4096]{1,0:T(8,128)}) %reduce-scatter.2.cloned.1.call-update) | async-done | bytes 131088 | tf_op jit(solution)/shard_map/reduce_scatter | solution.py:55
  218.3 29.1 %convolution_convert_fusion = bf16[1,128,4096]{2,0,1:T(2,128)(2,1)S(1)} fusion(bf16[1,255,4096]{2,1,0:T(8,128)(2,1)S(1)} %copy-done.2, bf16[128,1,4096]{2,0,1:T(8,128)(2,1)} %dynamic-slice_bitcast_fusion), kind=kOutput, calls=%fused_computation | convolution fusion | flops 134742016 | bytes 4186112 | tf_op jit(solution)/shard_map/conv_general_dilated | solution.py:32
  247.5 2.1 copy.12
  249.6 1.6 broadcast_multiply_fusion
  (89 shorter events, 9.9 us)
Async XLA Ops:
  7.2 114.5 %copy-start = (bf16[1,128,4096]{2,1,0:T(8,128)(2,1)S(1)}, bf16[1,128,4096]{2,1,0:T(8,128)(2,1)}, u32[]{:S(2)}) copy-start(bf16[1,128,4096]{2,1,0:T(8,128)(2,1)} %param.4) | copy-start | bytes 3145732
  7.2 211.1 %reduce-scatter.2.cloned.1.call-start = ((), (), s32[]{:S(2)}) async-start(), calls=%async_computation.1 | async-start | bytes 2228224 | tf_op jit(solution)/shard_map/reduce_scatter | solution.py:55
  7.2 7.7 %collective-permute-start.1 = (bf16[8,4096]{1,0:T(8,128)(2,1)}, bf16[8,4096]{1,0:T(8,128)(2,1)S(1)}, u32[]{:S(2)}, u32[]{:S(2)}) collective-permute-start(bf16[8,4096]{1,0:T(8,128)(2,1)} %param.7), channel_id=1, source_target_pairs={{0,2},{2,4},{4,6},{6,8},{8,10},{10,12},{12,14},{14,16},{16,18},{18... | collective-permute-start | bytes 196616 | tf_op jit(solution)/shard_map/ppermute | solution.py:17
  14.9 6.4 %collective-permute-start.2 = (bf16[8,4096]{1,0:T(8,128)(2,1)S(1)}, bf16[8,4096]{1,0:T(8,128)(2,1)S(1)}, u32[]{:S(2)}, u32[]{:S(2)}) collective-permute-start(bf16[8,4096]{1,0:T(8,128)(2,1)S(1)} %collective-permute-done.1), channel_id=1, source_target_pairs={{0,2},{2,4},{4,6},{6,8},{8,10},{10,12},{12,14},{14,16},{16,18},{18... | collective-permute-start | bytes 196616 | tf_op jit(solution)/shard_map/ppermute | solution.py:17
  21.3 6.4 %collective-permute-start.3 = (bf16[8,4096]{1,0:T(8,128)(2,1)S(1)}, bf16[8,4096]{1,0:T(8,128)(2,1)S(1)}, u32[]{:S(2)}, u32[]{:S(2)}) collective-permute-start(bf16[8,4096]{1,0:T(8,128)(2,1)S(1)} %collective-permute-done.2), channel_id=1, source_target_pairs={{0,2},{2,4},{4,6},{6,8},{8,10},{10,12},{12,14},{14,16},{16,18},{18... | collective-permute-start | bytes 196616 | tf_op jit(solution)/shard_map/ppermute | solution.py:17
  27.7 6.4 %collective-permute-start.4 = (bf16[8,4096]{1,0:T(8,128)(2,1)S(1)}, bf16[8,4096]{1,0:T(8,128)(2,1)S(1)}, u32[]{:S(2)}, u32[]{:S(2)}) collective-permute-start(bf16[8,4096]{1,0:T(8,128)(2,1)S(1)} %collective-permute-done.3), channel_id=1, source_target_pairs={{0,2},{2,4},{4,6},{6,8},{8,10},{10,12},{12,14},{14,16},{16,18},{18... | collective-permute-start | bytes 196616 | tf_op jit(solution)/shard_map/ppermute | solution.py:17
  34.1 6.4 %collective-permute-start.5 = (bf16[8,4096]{1,0:T(8,128)(2,1)S(1)}, bf16[8,4096]{1,0:T(8,128)(2,1)S(1)}, u32[]{:S(2)}, u32[]{:S(2)}) collective-permute-start(bf16[8,4096]{1,0:T(8,128)(2,1)S(1)} %collective-permute-done.4), channel_id=1, source_target_pairs={{0,2},{2,4},{4,6},{6,8},{8,10},{10,12},{12,14},{14,16},{16,18},{18... | collective-permute-start | bytes 196616 | tf_op jit(solution)/shard_map/ppermute | solution.py:17
  40.5 6.4 %collective-permute-start.6 = (bf16[8,4096]{1,0:T(8,128)(2,1)S(1)}, bf16[8,4096]{1,0:T(8,128)(2,1)S(1)}, u32[]{:S(2)}, u32[]{:S(2)}) collective-permute-start(bf16[8,4096]{1,0:T(8,128)(2,1)S(1)} %collective-permute-done.5), channel_id=1, source_target_pairs={{0,2},{2,4},{4,6},{6,8},{8,10},{10,12},{12,14},{14,16},{16,18},{18... | collective-permute-start | bytes 196616 | tf_op jit(solution)/shard_map/ppermute | solution.py:17
  46.9 44.9 %copy-start.5 = (bf16[8,4096]{1,0:T(8,128)(2,1)}, bf16[8,4096]{1,0:T(8,128)(2,1)S(1)}, u32[]{:S(2)}) copy-start(bf16[8,4096]{1,0:T(8,128)(2,1)S(1)} %collective-permute-done.6) | copy-start | bytes 196612
  46.9 6.4 %collective-permute-start.7 = (bf16[8,4096]{1,0:T(8,128)(2,1)S(1)}, bf16[8,4096]{1,0:T(8,128)(2,1)S(1)}, u32[]{:S(2)}, u32[]{:S(2)}) collective-permute-start(bf16[8,4096]{1,0:T(8,128)(2,1)S(1)} %collective-permute-done.6), channel_id=1, source_target_pairs={{0,2},{2,4},{4,6},{6,8},{8,10},{10,12},{12,14},{14,16},{16,18},{18... | collective-permute-start | bytes 196616 | tf_op jit(solution)/shard_map/ppermute | solution.py:17
  53.2 38.3 %copy-start.7 = (bf16[8,4096]{1,0:T(8,128)(2,1)}, bf16[8,4096]{1,0:T(8,128)(2,1)S(1)}, u32[]{:S(2)}) copy-start(bf16[8,4096]{1,0:T(8,128)(2,1)S(1)} %collective-permute-done.7) | copy-start | bytes 196612
  53.2 6.4 %collective-permute-start.8 = (bf16[8,4096]{1,0:T(8,128)(2,1)S(1)}, bf16[8,4096]{1,0:T(8,128)(2,1)S(1)}, u32[]{:S(2)}, u32[]{:S(2)}) collective-permute-start(bf16[8,4096]{1,0:T(8,128)(2,1)S(1)} %collective-permute-done.7), channel_id=1, source_target_pairs={{0,2},{2,4},{4,6},{6,8},{8,10},{10,12},{12,14},{14,16},{16,18},{18... | collective-permute-start | bytes 196616 | tf_op jit(solution)/shard_map/ppermute | solution.py:17
  59.6 32.0 %copy-start.9 = (bf16[8,4096]{1,0:T(8,128)(2,1)}, bf16[8,4096]{1,0:T(8,128)(2,1)S(1)}, u32[]{:S(2)}) copy-start(bf16[8,4096]{1,0:T(8,128)(2,1)S(1)} %collective-permute-done.8) | copy-start | bytes 196612
  59.6 6.4 %collective-permute-start.9 = (bf16[8,4096]{1,0:T(8,128)(2,1)S(1)}, bf16[8,4096]{1,0:T(8,128)(2,1)S(1)}, u32[]{:S(2)}, u32[]{:S(2)}) collective-permute-start(bf16[8,4096]{1,0:T(8,128)(2,1)S(1)} %collective-permute-done.8), channel_id=1, source_target_pairs={{0,2},{2,4},{4,6},{6,8},{8,10},{10,12},{12,14},{14,16},{16,18},{18... | collective-permute-start | bytes 196616 | tf_op jit(solution)/shard_map/ppermute | solution.py:17
  66.0 25.6 %copy-start.11 = (bf16[8,4096]{1,0:T(8,128)(2,1)}, bf16[8,4096]{1,0:T(8,128)(2,1)S(1)}, u32[]{:S(2)}) copy-start(bf16[8,4096]{1,0:T(8,128)(2,1)S(1)} %collective-permute-done.9) | copy-start | bytes 196612
  66.0 6.4 %collective-permute-start.10 = (bf16[8,4096]{1,0:T(8,128)(2,1)S(1)}, bf16[8,4096]{1,0:T(8,128)(2,1)S(1)}, u32[]{:S(2)}, u32[]{:S(2)}) collective-permute-start(bf16[8,4096]{1,0:T(8,128)(2,1)S(1)} %collective-permute-done.9), channel_id=1, source_target_pairs={{0,2},{2,4},{4,6},{6,8},{8,10},{10,12},{12,14},{14,16},{16,18},{18... | collective-permute-start | bytes 196616 | tf_op jit(solution)/shard_map/ppermute | solution.py:17
  72.4 19.2 %copy-start.13 = (bf16[8,4096]{1,0:T(8,128)(2,1)}, bf16[8,4096]{1,0:T(8,128)(2,1)S(1)}, u32[]{:S(2)}) copy-start(bf16[8,4096]{1,0:T(8,128)(2,1)S(1)} %collective-permute-done.10) | copy-start | bytes 196612
  72.4 6.4 %collective-permute-start.11 = (bf16[8,4096]{1,0:T(8,128)(2,1)S(1)}, bf16[8,4096]{1,0:T(8,128)(2,1)S(1)}, u32[]{:S(2)}, u32[]{:S(2)}) collective-permute-start(bf16[8,4096]{1,0:T(8,128)(2,1)S(1)} %collective-permute-done.10), channel_id=1, source_target_pairs={{0,2},{2,4},{4,6},{6,8},{8,10},{10,12},{12,14},{14,16},{16,18},{18... | collective-permute-start | bytes 196616 | tf_op jit(solution)/shard_map/ppermute | solution.py:17
  78.8 6.4 %collective-permute-start.12 = (bf16[8,4096]{1,0:T(8,128)(2,1)S(1)}, bf16[8,4096]{1,0:T(8,128)(2,1)S(1)}, u32[]{:S(2)}, u32[]{:S(2)}) collective-permute-start(bf16[8,4096]{1,0:T(8,128)(2,1)S(1)} %collective-permute-done.11), channel_id=1, source_target_pairs={{0,2},{2,4},{4,6},{6,8},{8,10},{10,12},{12,14},{14,16},{16,18},{18... | collective-permute-start | bytes 196616 | tf_op jit(solution)/shard_map/ppermute | solution.py:17
  85.2 6.4 %collective-permute-start.13 = (bf16[8,4096]{1,0:T(8,128)(2,1)S(1)}, bf16[8,4096]{1,0:T(8,128)(2,1)S(1)}, u32[]{:S(2)}, u32[]{:S(2)}) collective-permute-start(bf16[8,4096]{1,0:T(8,128)(2,1)S(1)} %collective-permute-done.12), channel_id=1, source_target_pairs={{0,2},{2,4},{4,6},{6,8},{8,10},{10,12},{12,14},{14,16},{16,18},{18... | collective-permute-start | bytes 196616 | tf_op jit(solution)/shard_map/ppermute | solution.py:17
  91.6 6.5 %collective-permute-start.14 = (bf16[8,4096]{1,0:T(8,128)(2,1)S(1)}, bf16[8,4096]{1,0:T(8,128)(2,1)}, u32[]{:S(2)}, u32[]{:S(2)}) collective-permute-start(bf16[8,4096]{1,0:T(8,128)(2,1)S(1)} %collective-permute-done.13), channel_id=1, source_target_pairs={{0,2},{2,4},{4,6},{6,8},{8,10},{10,12},{12,14},{14,16},{16,18},{18... | collective-permute-start | bytes 196616 | tf_op jit(solution)/shard_map/ppermute | solution.py:17
  93.5 19.9 %copy-start.4 = (bf16[8,4096]{1,0:T(8,128)(2,1)S(1)}, bf16[8,4096]{1,0:T(8,128)(2,1)}, u32[]{:S(2)}) copy-start(bf16[8,4096]{1,0:T(8,128)(2,1)} %param.7) | copy-start | bytes 196612
  98.2 6.7 %collective-permute-start.15 = (bf16[8,4096]{1,0:T(8,128)(2,1)}, bf16[8,4096]{1,0:T(8,128)(2,1)}, u32[]{:S(2)}, u32[]{:S(2)}) collective-permute-start(bf16[8,4096]{1,0:T(8,128)(2,1)} %collective-permute-done.14), channel_id=1, source_target_pairs={{0,2},{2,4},{4,6},{6,8},{8,10},{10,12},{12,14},{14,16},{16,18},{18... | collective-permute-start | bytes 196616 | tf_op jit(solution)/shard_map/ppermute | solution.py:17
  98.3 22.0 %collective-permute-start = (bf16[127,4096]{1,0:T(8,128)(2,1)S(1)}, bf16[127,4096]{1,0:T(8,128)(2,1)}, u32[]{:S(2)}, u32[]{:S(2)}) collective-permute-start(bf16[127,4096]{1,0:T(8,128)(2,1)S(1)} %slice_bitcast_fusion), channel_id=1, source_target_pairs={{1,0},{3,2},{5,4},{7,6},{9,8},{11,10},{13,12},{15,14},{17,16},{19,... | collective-permute-start | bytes 3121160 | tf_op jit(solution)/shard_map/ppermute | solution.py:28
  99.7 15.5 %copy-start.14 = (bf16[8,4096]{1,0:T(8,128)(2,1)S(1)}, bf16[8,4096]{1,0:T(8,128)(2,1)}, u32[]{:S(2)}) copy-start(bf16[8,4096]{1,0:T(8,128)(2,1)} %copy-done.13) | copy-start | bytes 196612
  99.7 15.5 %copy-start.12 = (bf16[8,4096]{1,0:T(8,128)(2,1)S(1)}, bf16[8,4096]{1,0:T(8,128)(2,1)}, u32[]{:S(2)}) copy-start(bf16[8,4096]{1,0:T(8,128)(2,1)} %copy-done.11) | copy-start | bytes 196612
  99.7 15.6 %copy-start.10 = (bf16[8,4096]{1,0:T(8,128)(2,1)S(1)}, bf16[8,4096]{1,0:T(8,128)(2,1)}, u32[]{:S(2)}) copy-start(bf16[8,4096]{1,0:T(8,128)(2,1)} %copy-done.9) | copy-start | bytes 196612
  99.7 15.6 %copy-start.8 = (bf16[8,4096]{1,0:T(8,128)(2,1)S(1)}, bf16[8,4096]{1,0:T(8,128)(2,1)}, u32[]{:S(2)}) copy-start(bf16[8,4096]{1,0:T(8,128)(2,1)} %copy-done.7) | copy-start | bytes 196612
  99.7 15.6 %copy-start.6 = (bf16[8,4096]{1,0:T(8,128)(2,1)S(1)}, bf16[8,4096]{1,0:T(8,128)(2,1)}, u32[]{:S(2)}) copy-start(bf16[8,4096]{1,0:T(8,128)(2,1)} %copy-done.5) | copy-start | bytes 196612
  121.7 30.1 %copy-start.1 = (bf16[1,255,4096]{2,1,0:T(8,128)(2,1)}, bf16[1,255,4096]{2,1,0:T(8,128)(2,1)S(1)}, u32[]{:S(2)}) copy-start(bf16[1,255,4096]{2,1,0:T(8,128)(2,1)S(1)} %maximum_bitcast_fusion) | copy-start | bytes 6266884
  154.8 63.5 %copy-start.2 = (bf16[1,255,4096]{2,1,0:T(8,128)(2,1)S(1)}, bf16[1,255,4096]{2,1,0:T(8,128)(2,1)}, u32[]{:S(2)}) copy-start(bf16[1,255,4096]{2,1,0:T(8,128)(2,1)} %copy-done.1) | copy-start | bytes 6266884
  154.8 94.7 %all-reduce.2.cloned.1.call-start = ((), (), s32[]{:S(2)}) async-start(), calls=%async_computation.2 | async-start | bytes 262144 | tf_op jit(solution)/shard_map/psum | solution.py:54
  (7 other events, 77.4 us)
Sparse Core Ops, SparseCore 0:
  155.0 63.3 reduce-scatter.1
  220.6 20.4 all-reduce.1
